TPU v7x, 32 devices: a whole 2x2x4 slice. The times are simulated.
32 devices in a mesh: section: 4 (over y, x), seq: 8 (over z, core).
Axes of the slice: x: 2, y: 2, z: 4, core: 2. Of those that a mesh axis runs over, the one named last changes fastest.
Arguments:
- inputs: bfloat16 [4, 4096, 1536], P(None, 'seq'), may hold values from -40 to 40
- weights: bfloat16 [2, 5, 1536, 1536], P(None, None, None, 'section'), may hold values from -0.0625 to 0.0625
- gains: float32 [2, 1536], replicated, may hold values from 0.1 to 1.9
Outputs:
- activations: bfloat16 [2, 4, 4096, 1536], P(None, None, 'seq', 'section')
All inputs are finite; a program needn't handle non-finite values.
Results may differ from a plain program's by a relative error of at most 0.0044.
Values may be sent and summed in bfloat16 or wider, within the bound.
A program may use at most 128 MiB of HBM per device.

v0:
```python
import jax
import jax.numpy as jnp
from jax import lax
from jax.experimental import pallas as pl
from jax.experimental.pallas import tpu as pltpu
from jax.sharding import PartitionSpec as P

MESH = pl.DeviceIdType.MESH
HALO = 16
REACH = 2


def with_halo(value, sides, width):
    for axis, dim in sides:
        count, length = (lax.axis_size(axis), value.shape[dim])
        up = [(i, (i + 1) % count) for i in range(count - 1)]
        down = [(j, i) for i, j in up]
        last = lax.slice_in_dim(value, length - width, length, axis=dim)
        initial = lax.slice_in_dim(value, 0, width, axis=dim)
        before = lax.ppermute(last, axis, up)
        after = lax.ppermute(initial, axis, down)
        value = jnp.concatenate([before, value, after], axis=dim)
    return value


def convolve(padded, kernel):
    count = padded.shape[1] - 4
    total = jnp.zeros((padded.shape[0], count, kernel.shape[2]), jnp.float32)
    for k in range(5):
        total = total + jnp.einsum(
            "brc,co->bro", padded[:, k : k + count], kernel[k], preferred_element_type=jnp.float32
        )
    return total


def normed(current, gain):
    values = current.astype(jnp.float32)
    scale = lax.rsqrt(jnp.mean(values * values, axis=-1, keepdims=True) + 1e-06)
    return jax.nn.gelu(values * scale * gain).astype(jnp.bfloat16)


def neighbours(hidden):
    return with_halo(hidden, (("seq", 1),), 2)


def plain(inputs, weights, gains):
    share = weights.shape[3]
    begin = lax.axis_index("section") * share
    hidden = normed(inputs, gains[0])
    conv = convolve(neighbours(hidden), weights[0])
    own = lax.dynamic_slice_in_dim(inputs, begin, share, 2)
    current = (own.astype(jnp.float32) + conv).astype(jnp.bfloat16)
    results = [current]
    kernel = weights[1]
    whole = lax.all_gather(current, "section", axis=2, tiled=True)
    conv = convolve(neighbours(normed(whole, gains[1])), kernel)
    current = (current.astype(jnp.float32) + conv).astype(jnp.bfloat16)
    results.append(current)
    return jnp.stack(results, axis=0)


def gelu(v):
    return 0.5 * v * (1.0 + jnp.tanh(v * (0.7978845608028654 + 0.035677408136300125 * (v * v))))


def fused_kernel(
    x, w, g, out, xe, hid, y, wv, acts, last, wsem, xsem, hsend, hrecv, ssem, rsem, osem
):
    micro, rows, chans = x.shape
    taps, share = w.shape[1], w.shape[3]
    span = rows + 2 * HALO
    half = span // 2
    trim = half - HALO // 2
    part = trim // 16 * 8
    me, seq = lax.axis_index("section"), lax.axis_index("seq")
    nseq = lax.axis_size("seq")

    def ring(at):
        r = at // 2
        return 2 * r + (at % 2) * (1 - 2 * (r % 2)) + r % 2

    place = ring(me)
    right, left = ring((place + 1) % 4), ring((place + 3) % 4)
    over = ring((place + 2) % 4)

    def load(b):
        return pltpu.make_async_copy(x.at[b], xe.at[b, pl.ds(HALO, rows)], xsem.at[b])

    def weight(l, k):
        return pltpu.make_async_copy(w.at[l, k], wv.at[l, :, pl.ds(k * share, share)], wsem.at[l, k])

    load(0).start()
    for k in range(taps):
        weight(0, k).start()

    barrier = pltpu.get_barrier_semaphore()
    for to in (right, left):
        pl.semaphore_signal(barrier, inc=1, device_id=(to, seq), device_id_type=MESH)

    @pl.when(seq > 0)
    def _():
        pl.semaphore_signal(barrier, inc=1, device_id=(me, seq - 1), device_id_type=MESH)

    @pl.when(seq < nseq - 1)
    def _():
        pl.semaphore_signal(barrier, inc=1, device_id=(me, seq + 1), device_id_type=MESH)

    peers = 2 + jnp.where(seq > 0, 1, 0) + jnp.where(seq < nseq - 1, 1, 0)
    pl.semaphore_wait(barrier, peers)

    def halo_up(b):
        return pltpu.make_async_remote_copy(
            src_ref=x.at[b, pl.ds(rows - HALO, HALO), :],
            dst_ref=xe.at[b, pl.ds(0, HALO), :],
            send_sem=hsend.at[0, b],
            recv_sem=hrecv.at[0, b],
            device_id=(me, seq + 1),
            device_id_type=MESH,
        )

    def halo_down(b):
        return pltpu.make_async_remote_copy(
            src_ref=x.at[b, pl.ds(0, HALO), :],
            dst_ref=xe.at[b, pl.ds(HALO + rows, HALO), :],
            send_sem=hsend.at[1, b],
            recv_sem=hrecv.at[1, b],
            device_id=(me, seq - 1),
            device_id_type=MESH,
        )

    @pl.when(seq < nseq - 1)
    def _():
        for b in range(micro):
            halo_up(b).start()

    @pl.when(seq > 0)
    def _():
        for b in range(micro):
            halo_down(b).start()

    @pl.when(seq == 0)
    def _():
        xe[:, 0:HALO, :] = jnp.zeros((micro, HALO, chans), jnp.bfloat16)

    @pl.when(seq == nseq - 1)
    def _():
        xe[:, HALO + rows : span, :] = jnp.zeros((micro, HALO, chans), jnp.bfloat16)

    for l in range(2):
        y[l, 0:8, :] = jnp.zeros((8, taps * share), jnp.float32)
        y[l, span + 8 : span + 16, :] = jnp.zeros((8, taps * share), jnp.float32)

    def piece(origin, b, start, size):
        return acts.at[origin, b, pl.ds(start, size), :]

    def send(origin, b, start, size, way, c, to):
        return pltpu.make_async_remote_copy(
            src_ref=piece(origin, b, start, size),
            dst_ref=piece(origin, b, start, size),
            send_sem=ssem.at[way, c],
            recv_sem=rsem.at[way, c],
            device_id=(to, seq),
            device_id_type=MESH,
        )

    def start(h):
        return HALO // 2 + h * trim

    def direct(b, h):
        c = 2 * b + h
        send(me, b, start(h), trim, 0, c, right).start()
        send(me, b, start(h), trim, 1, c, left).start()

    def forward(b, h):
        c = 2 * b + h
        send(left, b, start(h), trim, 0, c, left).wait_recv()
        send(left, b, start(h), part, 2, c, right).start()
        send(right, b, start(h), trim, 1, c, right).wait_recv()
        send(right, b, start(h) + part, trim - part, 3, c, left).start()

    def arrived(b, h):
        c = 2 * b + h
        send(over, b, start(h), part, 2, c, left).wait_recv()
        send(over, b, start(h) + part, trim - part, 3, c, right).wait_recv()

    tile = 16

    def normalize(read, l, begin, end):
        gain = g[l : l + 1, :]

        @pl.loop(0, (end - begin) // tile, unroll=True)
        def _(i):
            at = pl.multiple_of(begin + i * tile, tile)
            v = read(at)
            scale = lax.rsqrt(jnp.mean(v * v, axis=-1, keepdims=True) + 1e-06)
            hid[l, pl.ds(at, tile), :] = gelu(v * scale * gain).astype(jnp.bfloat16)

    def multiply(l, begin, end):
        wide = taps * share
        step = 512
        for n in range(0, wide, step):
            size = min(step, wide - n)
            y[l, begin + 8 : end + 8, n : n + size] = jnp.dot(
                hid[l, begin:end, :], wv[l, :, n : n + size], preferred_element_type=jnp.float32
            )

    def combine(l, begin, end, residual, store):
        @pl.loop(0, (end - begin) // tile, unroll=True)
        def _(i):
            at = pl.multiple_of(begin + i * tile, tile)
            total = None
            for k in range(taps):
                block = y[l, pl.ds(at, tile + 16), k * share : (k + 1) * share]
                term = block[8 - REACH + k : 8 - REACH + k + tile, :]
                total = term if total is None else total + term
            store(at, residual(at) + total)

    low = jnp.where(seq == 0, HALO, 0)
    high = jnp.where(seq == nseq - 1, HALO + rows, span)
    mine = pl.ds(pl.multiple_of(me * share, 128), share)

    def first(b, h):
        def read(at):
            return xe[b, pl.ds(at, tile), :].astype(jnp.float32)

        def residual(at):
            return xe[b, pl.ds(at, tile), mine].astype(jnp.float32)

        def store(at, value):
            row = at + lax.broadcasted_iota(jnp.int32, value.shape, 0)
            value = jnp.where((row >= low) & (row < high), value, 0.0)
            acts[me, b, pl.ds(at, tile), :] = value.astype(jnp.bfloat16)

        begin, end = ((0, half + HALO), (half + HALO, span))[h]
        normalize(read, 0, begin, end)
        multiply(0, begin, end)
        combine(0, h * half, h * half + half, residual, store)

    def second(b, h):
        def read(at):
            parts = [acts[s, b, pl.ds(at, tile), :].astype(jnp.float32) for s in range(4)]
            return jnp.concatenate(parts, axis=-1)

        def residual(at):
            return acts[me, b, pl.ds(at, tile), :].astype(jnp.float32)

        def store(at, value):
            last[b, pl.ds(pl.multiple_of(at - HALO, tile), tile), :] = value.astype(jnp.bfloat16)

        normalize(read, 1, h * half, h * half + half)
        multiply(1, h * half, h * half + half)
        cut = half - HALO
        begin, end = ((HALO, cut), (cut, HALO + rows))[h]
        combine(1, begin, end, residual, store)

    def out_first(b):
        return pltpu.make_async_copy(
            acts.at[me, b, pl.ds(HALO, rows), :], out.at[0, b], osem.at[0, b]
        )

    def out_last(b):
        return pltpu.make_async_copy(last.at[b], out.at[1, b], osem.at[1, b])

    def weights_ready(l):
        for k in range(taps):
            weight(l, k).wait()

    @pl.loop(0, micro + 1)
    def _(b):
        @pl.when(b < micro)
        def _():
            load(b).wait()

            @pl.when(seq > 0)
            def _():
                halo_up(b).wait_recv()

            @pl.when(b == 0)
            def _():
                weights_ready(0)
                for other in range(1, micro):
                    load(other).start()
                for k in range(taps):
                    weight(1, k).start()

            first(b, 0)
            direct(b, 0)

        @pl.when(b > 0)
        def _():
            forward(b - 1, 1)
            arrived(b - 1, 0)

            @pl.when(b == 1)
            def _():
                weights_ready(1)

            second(b - 1, 0)

        @pl.when(b < micro)
        def _():
            @pl.when(seq < nseq - 1)
            def _():
                halo_down(b).wait_recv()

            first(b, 1)
            direct(b, 1)
            out_first(b).start()
            forward(b, 0)

        @pl.when(b > 0)
        def _():
            arrived(b - 1, 1)
            second(b - 1, 1)
            out_last(b - 1).start()

    @pl.when(seq < nseq - 1)
    def _():
        for b in range(micro):
            halo_up(b).wait_send()

    @pl.when(seq > 0)
    def _():
        for b in range(micro):
            halo_down(b).wait_send()

    @pl.loop(0, micro)
    def _(b):
        out_first(b).wait()
        out_last(b).wait()
        for h in range(2):
            c = 2 * b + h
            send(me, b, start(h), trim, 0, c, right).wait_send()
            send(me, b, start(h), trim, 1, c, left).wait_send()
            send(left, b, start(h), part, 2, c, right).wait_send()
            send(right, b, start(h) + part, trim - part, 3, c, left).wait_send()


def fused(inputs, weights, gains):
    micro, rows, chans = inputs.shape
    layers, taps, _, share = weights.shape
    span = rows + 2 * HALO
    chunks = 2 * micro
    dma = pltpu.SemaphoreType.DMA
    hbm = pl.BlockSpec(memory_space=pltpu.HBM)
    return pl.pallas_call(
        fused_kernel,
        out_shape=jax.ShapeDtypeStruct((layers, micro, rows, share), jnp.bfloat16),
        in_specs=[hbm, hbm, pl.BlockSpec(memory_space=pltpu.VMEM)],
        out_specs=pl.BlockSpec(memory_space=pl.ANY),
        scratch_shapes=[
            pltpu.VMEM((micro, span, chans), jnp.bfloat16),
            pltpu.VMEM((2, span, chans), jnp.bfloat16),
            pltpu.VMEM((2, span + 16, taps * share), jnp.float32),
            pltpu.VMEM((2, chans, taps * share), jnp.bfloat16),
            pltpu.VMEM((4, micro, span, share), jnp.bfloat16),
            pltpu.VMEM((micro, rows, share), jnp.bfloat16),
            dma((2, taps)),
            dma((micro,)),
            dma((2, micro)),
            dma((2, micro)),
            dma((4, chunks)),
            dma((4, chunks)),
            dma((2, micro)),
        ],
        compiler_params=pltpu.CompilerParams(
            collective_id=0, has_side_effects=True, vmem_limit_bytes=50 * 1024 * 1024
        ),
    )(inputs, weights, gains)


def local(inputs, weights, gains):
    square = lax.axis_size("section") == 4 and weights.shape[0] == 2
    if square and weights.shape[3] % 128 == 0 and inputs.shape[1] % 32 == 0:
        return fused(inputs, weights, gains)
    return plain(inputs, weights, gains)


def solution(mesh):
    in_specs = (P(None, "seq", None), P(None, None, None, "section"), P())
    out_specs = P(None, None, "seq", "section")
    return jax.shard_map(local, mesh=mesh, in_specs=in_specs, out_specs=out_specs, check_vma=False)
```

profile of v0, /device:TPU:0, one launch (start us, length us, event | category | flops | bytes accessed | tf_op | source)
XLA Modules:
  0.0 68.9 jit_solution(9417321126139837298)
XLA Ops:
  0.0 0.0 copy-start
  0.0 0.7 %copy-done = f32[2,1536]{1,0:T(2,128)S(1)} copy-done((f32[2,1536]{1,0:T(2,128)S(1)}, f32[2,1536]{1,0:T(2,128)}, u32[]{:S(2)}) %copy-start) | copy-done | bytes 12312
  0.7 66.5 %shard_map.37 = bf16[2,4,512,384]{3,2,1,0:T(8,128)(2,1)S(1)} custom-call(bf16[4,512,1536]{2,1,0:T(8,128)(2,1)} %x.1, bf16[2,5,1536,384]{3,2,1,0:T(8,128)(2,1)} %w.1, f32[2,1536]{1,0:T(2,128)S(1)} %copy-done), custom_call_target="tpu_custom_call" | custom-call | tf_op jit(solution)/shard_map/pallas_call | solution.py:346
  67.2 1.7 %copy.5 = bf16[2,4,512,384]{3,2,1,0:T(8,128)(2,1)} copy(bf16[2,4,512,384]{3,2,1,0:T(8,128)(2,1)S(1)} %shard_map.37) | data formatting | bytes 6291456
Async XLA Ops:
  0.0 0.7 %copy-start = (f32[2,1536]{1,0:T(2,128)S(1)}, f32[2,1536]{1,0:T(2,128)}, u32[]{:S(2)}) copy-start(f32[2,1536]{1,0:T(2,128)} %g.1) | copy-start | bytes 36868
where the time goes:
time: 69.1 us; the launch traced here: 68.9 us
  Pallas kernels  66.5 us (96%)
  local copies, waits for them, and re-layouts  2.37 us (3%)
    pallas_call x1, Pallas kernels, fused(): pl.pallas_call(fused_kernel, out_shape=jax.ShapeDtypeStruct((layers, micr...  66.5 us
    unnamed x3, local copies, waits for them, and re-layouts  2.37 us

commit v1 on v0

v1 whole, which is shorter than its diff:
```python
import jax
import jax.numpy as jnp
from jax import lax
from jax.experimental import pallas as pl
from jax.experimental.pallas import tpu as pltpu
from jax.sharding import PartitionSpec as P

MESH = pl.DeviceIdType.MESH
HALO = 16
REACH = 2
EXTRA = 128


def with_halo(value, sides, width):
    for axis, dim in sides:
        count, length = (lax.axis_size(axis), value.shape[dim])
        up = [(i, (i + 1) % count) for i in range(count - 1)]
        down = [(j, i) for i, j in up]
        last = lax.slice_in_dim(value, length - width, length, axis=dim)
        initial = lax.slice_in_dim(value, 0, width, axis=dim)
        before = lax.ppermute(last, axis, up)
        after = lax.ppermute(initial, axis, down)
        value = jnp.concatenate([before, value, after], axis=dim)
    return value


def convolve(padded, kernel):
    count = padded.shape[1] - 4
    total = jnp.zeros((padded.shape[0], count, kernel.shape[2]), jnp.float32)
    for k in range(5):
        total = total + jnp.einsum(
            "brc,co->bro", padded[:, k : k + count], kernel[k], preferred_element_type=jnp.float32
        )
    return total


def normed(current, gain):
    values = current.astype(jnp.float32)
    scale = lax.rsqrt(jnp.mean(values * values, axis=-1, keepdims=True) + 1e-06)
    return jax.nn.gelu(values * scale * gain).astype(jnp.bfloat16)


def neighbours(hidden):
    return with_halo(hidden, (("seq", 1),), 2)


def plain(inputs, weights, gains):
    share = weights.shape[3]
    begin = lax.axis_index("section") * share
    hidden = normed(inputs, gains[0])
    conv = convolve(neighbours(hidden), weights[0])
    own = lax.dynamic_slice_in_dim(inputs, begin, share, 2)
    current = (own.astype(jnp.float32) + conv).astype(jnp.bfloat16)
    results = [current]
    kernel = weights[1]
    whole = lax.all_gather(current, "section", axis=2, tiled=True)
    conv = convolve(neighbours(normed(whole, gains[1])), kernel)
    current = (current.astype(jnp.float32) + conv).astype(jnp.bfloat16)
    results.append(current)
    return jnp.stack(results, axis=0)


def gelu(v):
    return 0.5 * v * (1.0 + jnp.tanh(v * (0.7978845608028654 + 0.035677408136300125 * (v * v))))


def chunk_ends(rows):
    tiles = rows // 16
    return [tiles * 11 // 32 * 16, tiles * 23 // 32 * 16, rows]


def schedule(count):
    early = {4 + 3 * m: m for m in range(count) if 4 + 3 * m < count}
    between = list(range(len(early), min(len(early) + 2, count)))
    rest = range(len(early) + len(between), count)
    late = {}
    for n, m in enumerate(rest):
        late.setdefault(max(0, min(2 * n + 1, m - 1)), []).append(m)
    return early, between, late


def fused_kernel(
    x, w, g, out, xe, hid, hid1, y, yx, wv, wx, gv, acts, last,
    gsem, wsem, xsem, hsend, hrecv, ssem, rsem, osem, lsem,
    tsend, trecv, zsend, zrecv, psend, precv,
):
    micro, rows, chans = x.shape
    taps, share = w.shape[1], w.shape[3]
    span = rows + 2 * HALO
    ends = chunk_ends(rows)
    begins = [0] + ends[:-1]
    parts = len(ends)
    count = parts * micro
    me, seq = lax.axis_index("section"), lax.axis_index("seq")
    nseq = lax.axis_size("seq")
    planes = nseq // 2
    plane, core = seq // 2, seq % 2
    partner = seq + 1 - 2 * core
    piece_rows = chans // nseq
    early, between, late = schedule(count)

    def ring(at):
        r = at // 2
        return 2 * r + (at % 2) * (1 - 2 * (r % 2)) + r % 2

    place = ring(me)
    right, left = ring((place + 1) % 4), ring((place + 3) % 4)
    over = ring((place + 2) % 4)

    gains = pltpu.make_async_copy(g, gv, gsem)

    def load(b):
        return pltpu.make_async_copy(x.at[b], xe.at[b, pl.ds(HALO, rows)], xsem.at[b])

    def weight(l, k):
        return pltpu.make_async_copy(w.at[l, k], wv.at[l, :, pl.ds(k * share, share)], wsem.at[l, k])

    gains.start()
    load(0).start()
    for k in range(taps):
        weight(0, k).start()

    barrier = pltpu.get_barrier_semaphore()
    for to in (right, left):
        pl.semaphore_signal(barrier, inc=1, device_id=(to, seq), device_id_type=MESH)

    def greet(reach):
        @pl.when(seq >= reach)
        def _():
            pl.semaphore_signal(barrier, inc=1, device_id=(me, seq - reach), device_id_type=MESH)

        @pl.when(seq < nseq - reach)
        def _():
            pl.semaphore_signal(barrier, inc=1, device_id=(me, seq + reach), device_id_type=MESH)

    greet(1)
    greet(2)
    peers = 2
    for reach in (1, 2):
        peers = peers + jnp.where(seq >= reach, 1, 0) + jnp.where(seq < nseq - reach, 1, 0)
    pl.semaphore_wait(barrier, peers)

    def halo_up(b):
        return pltpu.make_async_remote_copy(
            src_ref=x.at[b, pl.ds(rows - HALO, HALO), :],
            dst_ref=xe.at[b, pl.ds(0, HALO), :],
            send_sem=hsend.at[0, b],
            recv_sem=hrecv.at[0, b],
            device_id=(me, seq + 1),
            device_id_type=MESH,
        )

    def halo_down(b):
        return pltpu.make_async_remote_copy(
            src_ref=x.at[b, pl.ds(0, HALO), :],
            dst_ref=xe.at[b, pl.ds(HALO + rows, HALO), :],
            send_sem=hsend.at[1, b],
            recv_sem=hrecv.at[1, b],
            device_id=(me, seq - 1),
            device_id_type=MESH,
        )

    def tap(k):
        return pltpu.make_async_remote_copy(
            src_ref=w.at[0, k, pl.ds(seq * piece_rows, piece_rows), pl.ds(0, EXTRA)],
            dst_ref=wx.at[pl.ds(seq * piece_rows, piece_rows), pl.ds(k * EXTRA, EXTRA)],
            send_sem=tsend.at[k],
            recv_sem=trecv.at[k],
            device_id=(right, seq),
            device_id_type=MESH,
        )

    groups = ((0, 3), (3, taps))

    def block(index, n):
        low, high = groups[n]
        return wx.at[
            pl.ds(pl.multiple_of(index * piece_rows, 8), piece_rows),
            pl.ds(low * EXTRA, (high - low) * EXTRA),
        ]

    def spread(at, n, way, to):
        source = 2 * at + core
        return pltpu.make_async_remote_copy(
            src_ref=block(source, n),
            dst_ref=block(source, n),
            send_sem=zsend.at[way, at, n],
            recv_sem=zrecv.at[at, n],
            device_id=(me, to),
            device_id_type=MESH,
        )

    def swap(at, n):
        source = 2 * at + core
        return pltpu.make_async_remote_copy(
            src_ref=block(source, n),
            dst_ref=block(source, n),
            send_sem=psend.at[at, n],
            recv_sem=precv.at[at, n],
            device_id=(me, partner),
            device_id_type=MESH,
        )

    def swapped(at, n):
        source = 2 * at + 1 - core
        return pltpu.make_async_remote_copy(
            src_ref=block(source, n),
            dst_ref=block(source, n),
            send_sem=psend.at[at, n],
            recv_sem=precv.at[at, n],
            device_id=(me, partner),
            device_id_type=MESH,
        )

    def spread_own(n):
        for k in range(*groups[n]):
            tap(k).wait_recv()

        @pl.when(plane < planes - 1)
        def _():
            spread(plane, n, 0, seq + 2).start()

        @pl.when(plane > 0)
        def _():
            spread(plane, n, 1, seq - 2).start()

        swap(plane, n).start()

    def spread_far(d, n):
        @pl.when(plane >= d)
        def _():
            spread(plane - d, n, 0, seq).wait_recv()

            @pl.when(plane < planes - 1)
            def _():
                spread(plane - d, n, 0, seq + 2).start()

            swap(plane - d, n).start()

        @pl.when(plane < planes - d)
        def _():
            spread(plane + d, n, 1, seq).wait_recv()

            @pl.when(plane > 0)
            def _():
                spread(plane + d, n, 1, seq - 2).start()

            swap(plane + d, n).start()

    def spread_sent():
        for n in range(len(groups)):
            for k in range(*groups[n]):
                tap(k).wait_send()
            for at in range(planes):
                swap(at, n).wait_send()

                @pl.when((plane >= at) & (plane < planes - 1))
                def _():
                    spread(at, n, 0, seq + 2).wait_send()

                @pl.when((plane <= at) & (plane > 0))
                def _():
                    spread(at, n, 1, seq - 2).wait_send()

    @pl.when(seq < nseq - 1)
    def _():
        for b in range(micro):
            halo_up(b).start()

    @pl.when(seq > 0)
    def _():
        for b in range(micro):
            halo_down(b).start()

    for k in range(taps):
        tap(k).start()

    @pl.when(seq == 0)
    def _():
        xe[:, 0:HALO, :] = jnp.zeros((micro, HALO, chans), jnp.bfloat16)

    @pl.when(seq == nseq - 1)
    def _():
        xe[:, HALO + rows : span, :] = jnp.zeros((micro, HALO, chans), jnp.bfloat16)

    def send(origin, c, way, to):
        b, t = c // parts, c % parts
        size = ends[t] - begins[t] + (8 if t == parts - 1 else 0)
        low, high = ((EXTRA, share), (0, share), (EXTRA, share), (0, EXTRA))[way]
        ref = acts.at[origin, b, pl.ds(begins[t], size), pl.ds(low, high - low)]
        return pltpu.make_async_remote_copy(
            src_ref=ref,
            dst_ref=ref,
            send_sem=ssem.at[way, c],
            recv_sem=rsem.at[way, c],
            device_id=(to, seq),
            device_id_type=MESH,
        )

    def direct(c):
        send(me, c, 0, right).start()
        send(me, c, 1, left).start()

    def forward(c):
        send(left, c, 0, left).wait_recv()
        send(left, c, 2, right).start()
        send(right, c, 1, right).wait_recv()
        send(right, c, 3, left).start()
        if c + 3 < count:
            direct(c + 3)

    def arrived(b, t):
        size = ends[t] - begins[t] + (8 if t == parts - 1 else 0)
        c = b * parts + t
        for way, low, high in ((2, EXTRA, share), (3, 0, EXTRA)):
            ref = acts.at[over, b, pl.ds(begins[t], size), pl.ds(low, high - low)]
            pltpu.make_async_remote_copy(
                src_ref=ref,
                dst_ref=ref,
                send_sem=ssem.at[way, c],
                recv_sem=rsem.at[way, c],
                device_id=(right, seq),
                device_id_type=MESH,
            ).wait_recv()

    tile = 16

    def activate(v, l):
        scale = lax.rsqrt(jnp.mean(v * v, axis=-1, keepdims=True) + 1e-06)
        return gelu(v * scale * gv[l : l + 1, :]).astype(jnp.bfloat16)

    def merged(b, columns):
        top = xe[b, 0:HALO, columns].astype(jnp.float32)[8:16, :]
        bottom = xe[b, HALO + rows : span, columns].astype(jnp.float32)[0:8, :]
        row = lax.broadcasted_iota(jnp.int32, top.shape, 0)
        return jnp.where(row < 4, bottom, top)

    def product(dst, src, kernel, at, begin, end, wide, ready=None):
        step = 512
        for n in range(0, wide, step):
            size = min(step, wide - n)
            if ready is not None:
                ready(n, n + size)
            dst[begin + at : end + at, n : n + size] = jnp.dot(
                src(begin, end), kernel(n, size), preferred_element_type=jnp.float32
            )

    def gather_taps(src, at, width, stride):
        total = None
        block = src[pl.ds(pl.multiple_of(at + 16, 8), tile + 16), :]
        for k in range(taps):
            term = block[8 - REACH + k : 8 - REACH + k + tile, k * stride : k * stride + width]
            total = term if total is None else total + term
        return total

    def each(begin, end, body):
        @pl.loop(0, (end - begin) // tile, unroll=True)
        def _(i):
            body(pl.multiple_of(begin + i * tile, tile))

    mine = pl.ds(pl.multiple_of(me * share, 128), share)
    theirs = pl.ds(pl.multiple_of(left * share, 128), EXTRA)

    def conv_first(b, t, src, owner, columns, width, stride):
        def body(at):
            value = xe[b, pl.ds(at + HALO, tile), columns].astype(jnp.float32)
            value = value + gather_taps(src, at, width, stride)
            acts[owner, b, pl.ds(at, tile), 0:width] = value.astype(jnp.bfloat16)

        each(begins[t], ends[t], body)
        if t == parts - 1:
            top = gather_taps(src, -8, width, stride)[0:8, :]
            bottom = gather_taps(src, rows - 8, width, stride)[8:16, :]
            row = lax.broadcasted_iota(jnp.int32, top.shape, 0)
            value = merged(b, columns) + jnp.where(row < 4, bottom, top)
            inside = ((row < 4) & (seq < nseq - 1)) | ((row >= 4) & (seq > 0))
            value = jnp.where(inside, value, 0.0)
            value = jnp.concatenate([value, jnp.zeros_like(value)], axis=0)
            acts[owner, b, rows : rows + 16, 0:width] = value.astype(jnp.bfloat16)

    def bounds(t):
        begin = 0 if t == 0 else ends[t - 1] + 2 * HALO
        end = HALO + rows if t == parts - 1 else ends[t] + 2 * HALO
        return begin, end

    def first(b, t):
        begin, end = bounds(t)
        if t == 0:
            load(b).wait()

            @pl.when(b == 0)
            def _():
                gains.wait()

        def own(at):
            hid[b, pl.ds(at, tile), :] = activate(xe[b, pl.ds(at, tile), :].astype(jnp.float32), 0)

        each(max(begin, HALO), end, own)
        if t == 0:

            @pl.when(seq > 0)
            def _():
                halo_up(b).wait_recv()

            @pl.when(seq < nseq - 1)
            def _():
                halo_down(b).wait_recv()

            edge = merged(b, slice(None))
            hid[b, 0:HALO, :] = activate(jnp.concatenate([jnp.zeros_like(edge), edge], axis=0), 0)

        def ready(low, high):
            @pl.when(b == 0)
            def _():
                for k in range(taps):
                    if low <= k * share < high:
                        weight(0, k).wait()

        product(
            y, lambda p, q: hid[b, p:q, :], lambda n, s: wv[0, :, n : n + s], 8, begin, end,
            taps * share, ready if t == 0 else None,
        )
        if t == 0:
            y[HALO + 8 + rows : HALO + 16 + rows, :] = y[HALO : HALO + 8, :]

            @pl.when(b == 0)
            def _():
                for other in range(1, micro):
                    load(other).start()
                for k in range(taps):
                    weight(1, k).start()

        conv_first(b, t, y, me, mine, share, share)

    def extra(b, t):
        begin, end = bounds(t)
        product(
            yx, lambda p, q: hid[b, p:q, :], lambda n, s: wx[:, n : n + s], 8, begin, end,
            taps * EXTRA,
        )
        if t == 0:
            yx[HALO + 8 + rows : HALO + 16 + rows, :] = yx[HALO : HALO + 8, :]
        conv_first(b, t, yx, left, theirs, EXTRA, EXTRA)

    def second(b, t):
        end = ends[t] + (HALO if t == parts - 1 else 0)

        def own(at):
            pieces = [acts[s, b, pl.ds(at, tile), :].astype(jnp.float32) for s in range(4)]
            hid1[pl.ds(at, tile), :] = activate(jnp.concatenate(pieces, axis=-1), 1)

        each(begins[t], ends[t], own)
        if t == parts - 1:
            pieces = [acts[s, b, rows : rows + HALO, :].astype(jnp.float32) for s in range(4)]
            edge = jnp.concatenate(pieces, axis=-1)[0:8, :]
            hid1[rows : rows + HALO, :] = activate(
                jnp.concatenate([edge, jnp.zeros_like(edge)], axis=0), 1
            )
        product(
            y, lambda p, q: hid1[p:q, :], lambda n, s: wv[1, :, n : n + s], 24, begins[t], end,
            taps * share,
        )
        if t == parts - 1:
            y[HALO : HALO + 8, :] = y[HALO + 8 + rows : HALO + 16 + rows, :]

        def body(at):
            value = acts[me, b, pl.ds(at, tile), :].astype(jnp.float32)
            value = value + gather_taps(y, at, share, share)
            last[b, pl.ds(at, tile), :] = value.astype(jnp.bfloat16)

        each(max(begins[t] - tile, tile), rows if t == parts - 1 else ends[t] - tile, body)
        if t == parts - 1:
            body(0)

    def out_first(b):
        return pltpu.make_async_copy(acts.at[me, b, pl.ds(0, rows), :], out.at[0, b], osem.at[b])

    cuts = (0, tile, ends[-2] - tile, rows)

    def out_last(b, n):
        part = pl.ds(cuts[n], cuts[n + 1] - cuts[n])
        return pltpu.make_async_copy(last.at[b, part], out.at[1, b, part], lsem.at[b, n])

    def at_step(b, t, table, act):
        for bb in range(micro):
            for m in table.get(bb * parts + t, ()):
                pl.when(b == bb)(lambda m=m: act(m))

    errands = {}
    for n in range(len(groups)):
        errands.setdefault(1 + 2 * n, []).append(("own", 0, n))
        for d in range(1, planes):
            errands.setdefault(min(5 + 4 * (d - 1) + n, count), []).append(("far", d, n))

    def errand(e):
        kind, d, n = e
        if kind == "own":
            spread_own(n)
        else:
            spread_far(d, n)

    @pl.loop(0, micro)
    def _(b):
        for t in range(parts):
            first(b, t)
            at_step(b, t, {c: (c,) for c in range(3)}, direct)
            at_step(b, t, {p: (m,) for p, m in early.items()}, forward)
            at_step(b, t, errands, errand)
        out_first(b).start()

    for m in between[:1]:
        forward(m)
    for e in errands.get(count, ()):
        errand(e)
    for m in between[1:]:
        forward(m)
    for n in range(len(groups)):
        for at in range(planes):
            swapped(at, n).wait_recv()
    for k in range(taps):
        weight(1, k).wait()

    @pl.loop(0, micro)
    def _(b):
        for t in range(parts):
            at_step(b, t, late, forward)
            extra(b, t)
            arrived(b, t)
            second(b, t)
            if t == parts - 2:
                out_last(b, 1).start()
        out_last(b, 0).start()
        out_last(b, 2).start()

    @pl.when(seq < nseq - 1)
    def _():
        for b in range(micro):
            halo_up(b).wait_send()

    @pl.when(seq > 0)
    def _():
        for b in range(micro):
            halo_down(b).wait_send()

    spread_sent()
    for c in range(count):
        send(me, c, 0, right).wait_send()
        send(me, c, 1, left).wait_send()
        send(left, c, 2, right).wait_send()
        send(right, c, 3, left).wait_send()

    @pl.loop(0, micro)
    def _(b):
        out_first(b).wait()
        for n in range(3):
            out_last(b, n).wait()


def fused(inputs, weights, gains):
    micro, rows, chans = inputs.shape
    layers, taps, _, share = weights.shape
    span = rows + 2 * HALO
    count = len(chunk_ends(rows)) * micro
    planes = lax.axis_size("seq") // 2
    dma = pltpu.SemaphoreType.DMA
    hbm = pl.BlockSpec(memory_space=pltpu.HBM)
    return pl.pallas_call(
        fused_kernel,
        out_shape=jax.ShapeDtypeStruct((layers, micro, rows, share), jnp.bfloat16),
        in_specs=[hbm, hbm, hbm],
        out_specs=pl.BlockSpec(memory_space=pl.ANY),
        scratch_shapes=[
            pltpu.VMEM((micro, span, chans), jnp.bfloat16),
            pltpu.VMEM((micro, rows + HALO, chans), jnp.bfloat16),
            pltpu.VMEM((rows + HALO, chans), jnp.bfloat16),
            pltpu.VMEM((rows + 40, taps * share), jnp.float32),
            pltpu.VMEM((rows + 40, taps * EXTRA), jnp.float32),
            pltpu.VMEM((2, chans, taps * share), jnp.bfloat16),
            pltpu.VMEM((chans, taps * EXTRA), jnp.bfloat16),
            pltpu.VMEM(gains.shape, jnp.float32),
            pltpu.VMEM((4, micro, rows + HALO, share), jnp.bfloat16),
            pltpu.VMEM((micro, rows, share), jnp.bfloat16),
            dma,
            dma((2, taps)),
            dma((micro,)),
            dma((2, micro)),
            dma((2, micro)),
            dma((4, count)),
            dma((4, count)),
            dma((micro,)),
            dma((micro, 3)),
            dma((taps,)),
            dma((taps,)),
            dma((2, planes, 2)),
            dma((planes, 2)),
            dma((planes, 2)),
            dma((planes, 2)),
        ],
        compiler_params=pltpu.CompilerParams(
            collective_id=0, has_side_effects=True, vmem_limit_bytes=50 * 1024 * 1024
        ),
    )(inputs, weights, gains)


def local(inputs, weights, gains):
    micro, rows, chans = inputs.shape
    layers, taps, _, share = weights.shape
    nseq = lax.axis_size("seq")
    square = lax.axis_size("section") == 4 and layers == 2 and nseq % 2 == 0 and nseq > 2
    wide = share % 128 == 0 and share > EXTRA and chans % (16 * nseq) == 0
    if square and wide and taps == 5 and micro > 1 and rows % 512 == 0:
        return fused(inputs, weights, gains)
    return plain(inputs, weights, gains)


def solution(mesh):
    in_specs = (P(None, "seq", None), P(None, None, None, "section"), P())
    out_specs = P(None, None, "seq", "section")
    return jax.shard_map(local, mesh=mesh, in_specs=in_specs, out_specs=out_specs, check_vma=False)
```

time: 69.1 us -> 70.3 us (1.017)
  Pallas kernels: 66.5 us -> 67.7 us
    pallas_call x1, Pallas kernels: 66.5 us -> 67.7 us  [fused(): pl.pallas_call(fused_kernel, out_shape=jax.ShapeDtypeStruct((layers, micr...]
where the time goes in v1:
time: 70.3 us; the launch traced here: 70.1 us
  Pallas kernels  67.7 us (96%)
  local copies, waits for them, and re-layouts  2.37 us (3%)
    pallas_call x1, Pallas kernels, fused(): pl.pallas_call(fused_kernel, out_shape=jax.ShapeDtypeStruct((layers, micr...  67.7 us
    unnamed x3, local copies, waits for them, and re-layouts  2.37 us

profile of v1, /device:TPU:0, one launch (start us, length us, event | category | flops | bytes accessed | tf_op | source)
XLA Modules:
  0.0 70.1 jit_solution(11096262781559292261)
XLA Ops:
  0.0 0.0 copy-start
  0.0 0.7 %copy-done = f32[2,1536]{1,0:T(2,128)S(1)} copy-done((f32[2,1536]{1,0:T(2,128)S(1)}, f32[2,1536]{1,0:T(2,128)}, u32[]{:S(2)}) %copy-start) | copy-done | bytes 12312
  0.7 67.7 %shard_map.37 = bf16[2,4,512,384]{3,2,1,0:T(8,128)(2,1)S(1)} custom-call(bf16[4,512,1536]{2,1,0:T(8,128)(2,1)} %x.1, bf16[2,5,1536,384]{3,2,1,0:T(8,128)(2,1)} %w.1, f32[2,1536]{1,0:T(2,128)S(1)} %copy-done), custom_call_target="tpu_custom_call" | custom-call | tf_op jit(solution)/shard_map/pallas_call | solution.py:567
  68.4 1.7 %copy.5 = bf16[2,4,512,384]{3,2,1,0:T(8,128)(2,1)} copy(bf16[2,4,512,384]{3,2,1,0:T(8,128)(2,1)S(1)} %shard_map.37) | data formatting | bytes 6291456
Async XLA Ops:
  0.0 0.7 %copy-start = (f32[2,1536]{1,0:T(2,128)S(1)}, f32[2,1536]{1,0:T(2,128)}, u32[]{:S(2)}) copy-start(f32[2,1536]{1,0:T(2,128)} %g.1) | copy-start | bytes 36868

commit v2 on v1

--- a/solution.py
+++ b/solution.py
@@ -1,3 +1,4 @@
+import functools
 import jax
 import jax.numpy as jnp
 from jax import lax
@@ -60,17 +61,17 @@
     return jnp.stack(results, axis=0)
 
 
-def gelu(v):
-    return 0.5 * v * (1.0 + jnp.tanh(v * (0.7978845608028654 + 0.035677408136300125 * (v * v))))
+def gelu_of_twice(h):
+    return h + h * jnp.tanh(h * (1.5957691216057308 + 0.285419265090401 * (h * h)))
 
 
 def chunk_ends(rows):
     tiles = rows // 16
-    return [tiles * 11 // 32 * 16, tiles * 23 // 32 * 16, rows]
+    return [tiles * 11 // 32 * 16, tiles * 23 // 32 * 16, rows + 8]
 
 
 def schedule(count):
-    early = {4 + 3 * m: m for m in range(count) if 4 + 3 * m < count}
+    early = {5 + 2 * m: m for m in range(3)}
     between = list(range(len(early), min(len(early) + 2, count)))
     rest = range(len(early) + len(between), count)
     late = {}
@@ -80,7 +81,7 @@
 
 
 def fused_kernel(
-    x, w, g, out, xe, hid, hid1, y, yx, wv, wx, gv, acts, last,
+    x, w, g, out, xe, hid_a, hid_b, hid_c, hid1, y, yx, wv, wx, gv, acts, last,
     gsem, wsem, xsem, hsend, hrecv, ssem, rsem, osem, lsem,
     tsend, trecv, zsend, zrecv, psend, precv,
 ):
@@ -115,10 +116,18 @@
     def weight(l, k):
         return pltpu.make_async_copy(w.at[l, k], wv.at[l, :, pl.ds(k * share, share)], wsem.at[l, k])
 
+    def load_part(n):
+        part = ((0, ends[0] + 64), (ends[0] + 64, rows))[n]
+        size = part[1] - part[0]
+        return pltpu.make_async_copy(
+            x.at[0, pl.ds(part[0], size)], xe.at[0, pl.ds(HALO + part[0], size)], xsem.at[n * micro]
+        )
+
     gains.start()
-    load(0).start()
+    load_part(0).start()
     for k in range(taps):
         weight(0, k).start()
+    load_part(1).start()
 
     barrier = pltpu.get_barrier_semaphore()
     for to in (right, left):
@@ -138,8 +147,6 @@
     peers = 2
     for reach in (1, 2):
         peers = peers + jnp.where(seq >= reach, 1, 0) + jnp.where(seq < nseq - reach, 1, 0)
-    pl.semaphore_wait(barrier, peers)
-
     def halo_up(b):
         return pltpu.make_async_remote_copy(
             src_ref=x.at[b, pl.ds(rows - HALO, HALO), :],
@@ -262,19 +269,6 @@
                 def _():
                     spread(at, n, 1, seq - 2).wait_send()
 
-    @pl.when(seq < nseq - 1)
-    def _():
-        for b in range(micro):
-            halo_up(b).start()
-
-    @pl.when(seq > 0)
-    def _():
-        for b in range(micro):
-            halo_down(b).start()
-
-    for k in range(taps):
-        tap(k).start()
-
     @pl.when(seq == 0)
     def _():
         xe[:, 0:HALO, :] = jnp.zeros((micro, HALO, chans), jnp.bfloat16)
@@ -283,9 +277,24 @@
     def _():
         xe[:, HALO + rows : span, :] = jnp.zeros((micro, HALO, chans), jnp.bfloat16)
 
+    def enter():
+        pl.semaphore_wait(barrier, peers)
+        for k in range(taps):
+            tap(k).start()
+
+        @pl.when(seq < nseq - 1)
+        def _():
+            for b in range(micro):
+                halo_up(b).start()
+
+        @pl.when(seq > 0)
+        def _():
+            for b in range(micro):
+                halo_down(b).start()
+
     def send(origin, c, way, to):
         b, t = c // parts, c % parts
-        size = ends[t] - begins[t] + (8 if t == parts - 1 else 0)
+        size = ends[t] - begins[t]
         low, high = ((EXTRA, share), (0, share), (EXTRA, share), (0, EXTRA))[way]
         ref = acts.at[origin, b, pl.ds(begins[t], size), pl.ds(low, high - low)]
         return pltpu.make_async_remote_copy(
@@ -310,7 +319,7 @@
             direct(c + 3)
 
     def arrived(b, t):
-        size = ends[t] - begins[t] + (8 if t == parts - 1 else 0)
+        size = ends[t] - begins[t]
         c = b * parts + t
         for way, low, high in ((2, EXTRA, share), (3, 0, EXTRA)):
             ref = acts.at[over, b, pl.ds(begins[t], size), pl.ds(low, high - low)]
@@ -327,155 +336,141 @@
 
     def activate(v, l):
         scale = lax.rsqrt(jnp.mean(v * v, axis=-1, keepdims=True) + 1e-06)
-        return gelu(v * scale * gv[l : l + 1, :]).astype(jnp.bfloat16)
-
-    def merged(b, columns):
-        top = xe[b, 0:HALO, columns].astype(jnp.float32)[8:16, :]
-        bottom = xe[b, HALO + rows : span, columns].astype(jnp.float32)[0:8, :]
-        row = lax.broadcasted_iota(jnp.int32, top.shape, 0)
-        return jnp.where(row < 4, bottom, top)
-
-    def product(dst, src, kernel, at, begin, end, wide, ready=None):
-        step = 512
-        for n in range(0, wide, step):
+        return gelu_of_twice(v * (0.5 * scale) * gv[l : l + 1, :]).astype(jnp.bfloat16)
+
+    step = 512
+
+    def product(dst, src, kernel, begin, end, wide, which=slice(None), beside=()):
+        starts = list(range(0, wide, step))[which]
+        for i, n in enumerate(starts):
+            for tile_work in beside[i :: len(starts)]:
+                tile_work()
             size = min(step, wide - n)
-            if ready is not None:
-                ready(n, n + size)
-            dst[begin + at : end + at, n : n + size] = jnp.dot(
+            dst[begin + 8 : end + 8, n : n + size] = jnp.dot(
                 src(begin, end), kernel(n, size), preferred_element_type=jnp.float32
             )
 
-    def gather_taps(src, at, width, stride):
+    def close(dst):
+        dst[0:8, :] = dst[rows + 16 : rows + 24, :]
+        dst[rows + 24 : rows + 32, :] = dst[8:16, :]
+
+    def gather_taps(src, u, width, stride):
         total = None
-        block = src[pl.ds(pl.multiple_of(at + 16, 8), tile + 16), :]
+        block = src[u : u + tile + 16, :]
         for k in range(taps):
             term = block[8 - REACH + k : 8 - REACH + k + tile, k * stride : k * stride + width]
             total = term if total is None else total + term
         return total
 
-    def each(begin, end, body):
-        @pl.loop(0, (end - begin) // tile, unroll=True)
-        def _(i):
-            body(pl.multiple_of(begin + i * tile, tile))
-
     mine = pl.ds(pl.multiple_of(me * share, 128), share)
     theirs = pl.ds(pl.multiple_of(left * share, 128), EXTRA)
 
+    def source(b, u, columns):
+        if u == rows - 16:
+            bottom = xe[b, HALO + rows : span, columns].astype(jnp.float32)
+            top = xe[b, 0:HALO, columns].astype(jnp.float32)
+            return jnp.concatenate([bottom[0:8, :], top[8:16, :]], axis=0)
+        at = HALO if u == rows else 2 * HALO + u
+        return xe[b, at : at + tile, columns].astype(jnp.float32)
+
+    edges0 = [0] + [e + 2 * tile for e in ends[:-1]] + [rows + 16]
+
+    hid = (hid_a, hid_b, hid_c)
+
+    def norm_first(b, t):
+        def work(u):
+            at = u - edges0[t]
+            hid[t][b, at : at + tile, :] = activate(source(b, u, slice(None)), 0)
+
+        return [functools.partial(work, u) for u in range(edges0[t], edges0[t + 1], tile)]
+
+    def outputs(edges, t):
+        begin = tile if t == 0 else edges[t] - tile
+        end = edges[t + 1] if t == parts - 1 else edges[t + 1] - tile
+        return list(range(begin, end, tile)) + ([0] if t == parts - 1 else [])
+
     def conv_first(b, t, src, owner, columns, width, stride):
-        def body(at):
-            value = xe[b, pl.ds(at + HALO, tile), columns].astype(jnp.float32)
-            value = value + gather_taps(src, at, width, stride)
-            acts[owner, b, pl.ds(at, tile), 0:width] = value.astype(jnp.bfloat16)
-
-        each(begins[t], ends[t], body)
+        for u in outputs(edges0, t):
+            value = source(b, u, columns) + gather_taps(src, u, width, stride)
+            at = u - tile
+            if u == rows - 16:
+                at = rows
+                row = lax.broadcasted_iota(jnp.int32, (8, width), 0)
+                value = jnp.where(row < 4, value[0:8, :], value[8:16, :])
+                inside = ((row < 4) & (seq < nseq - 1)) | ((row >= 4) & (seq > 0))
+                value = jnp.where(inside, value, 0.0)
+                value = jnp.concatenate([value, jnp.zeros_like(value)], axis=0)
+            elif u == rows:
+                at = rows - 32
+            elif u == 0:
+                at = rows - 16
+            acts[owner, b, at : at + tile, 0:width] = value.astype(jnp.bfloat16)
+
+    def multiply_first(b, t, which, beside=()):
+        product(
+            y, lambda p, q: hid[t][b], lambda n, s: wv[0, :, n : n + s],
+            edges0[t], edges0[t + 1], taps * share, which, beside,
+        )
+
+    def finish_first(b, t):
         if t == parts - 1:
-            top = gather_taps(src, -8, width, stride)[0:8, :]
-            bottom = gather_taps(src, rows - 8, width, stride)[8:16, :]
-            row = lax.broadcasted_iota(jnp.int32, top.shape, 0)
-            value = merged(b, columns) + jnp.where(row < 4, bottom, top)
-            inside = ((row < 4) & (seq < nseq - 1)) | ((row >= 4) & (seq > 0))
-            value = jnp.where(inside, value, 0.0)
-            value = jnp.concatenate([value, jnp.zeros_like(value)], axis=0)
-            acts[owner, b, rows : rows + 16, 0:width] = value.astype(jnp.bfloat16)
-
-    def bounds(t):
-        begin = 0 if t == 0 else ends[t - 1] + 2 * HALO
-        end = HALO + rows if t == parts - 1 else ends[t] + 2 * HALO
-        return begin, end
-
-    def first(b, t):
-        begin, end = bounds(t)
-        if t == 0:
-            load(b).wait()
-
-            @pl.when(b == 0)
-            def _():
-                gains.wait()
-
-        def own(at):
-            hid[b, pl.ds(at, tile), :] = activate(xe[b, pl.ds(at, tile), :].astype(jnp.float32), 0)
-
-        each(max(begin, HALO), end, own)
-        if t == 0:
-
-            @pl.when(seq > 0)
-            def _():
-                halo_up(b).wait_recv()
-
-            @pl.when(seq < nseq - 1)
-            def _():
-                halo_down(b).wait_recv()
-
-            edge = merged(b, slice(None))
-            hid[b, 0:HALO, :] = activate(jnp.concatenate([jnp.zeros_like(edge), edge], axis=0), 0)
-
-        def ready(low, high):
-            @pl.when(b == 0)
-            def _():
-                for k in range(taps):
-                    if low <= k * share < high:
-                        weight(0, k).wait()
-
+            close(y)
+        conv_first(b, t, y, me, mine, share, share)
+
+    head, tail = slice(0, 1), slice(1, None)
+
+    def extra(b, t, which, beside=()):
         product(
-            y, lambda p, q: hid[b, p:q, :], lambda n, s: wv[0, :, n : n + s], 8, begin, end,
-            taps * share, ready if t == 0 else None,
-        )
-        if t == 0:
-            y[HALO + 8 + rows : HALO + 16 + rows, :] = y[HALO : HALO + 8, :]
-
-            @pl.when(b == 0)
-            def _():
-                for other in range(1, micro):
-                    load(other).start()
-                for k in range(taps):
-                    weight(1, k).start()
-
-        conv_first(b, t, y, me, mine, share, share)
-
-    def extra(b, t):
-        begin, end = bounds(t)
+            yx, lambda p, q: hid[t][b], lambda n, s: wx[:, n : n + s],
+            edges0[t], edges0[t + 1], taps * EXTRA, which, beside,
+        )
+
+    def finish_extra(b, t):
+        if t == parts - 1:
+            close(yx)
+        conv_first(b, t, yx, left, theirs, EXTRA, EXTRA)
+
+    edges1 = [0] + ends[:-1] + [rows + 16]
+
+    def held(u):
+        return u if u < rows - 32 else rows if u == rows - 32 else u - 16
+
+    def norm_second(b, t):
+        def work(u):
+            at = held(u)
+            pieces = [acts[s, b, at : at + tile, :].astype(jnp.float32) for s in range(4)]
+            value = jnp.concatenate(pieces, axis=-1)
+            if at == rows:
+                value = jnp.concatenate([value[0:8, :], value[0:8, :]], axis=0)
+            hid1[u : u + tile, :] = activate(value, 1)
+
+        return [functools.partial(work, u) for u in range(edges1[t], edges1[t + 1], tile)]
+
+    def multiply_second(b, t, beside=()):
         product(
-            yx, lambda p, q: hid[b, p:q, :], lambda n, s: wx[:, n : n + s], 8, begin, end,
-            taps * EXTRA,
-        )
-        if t == 0:
-            yx[HALO + 8 + rows : HALO + 16 + rows, :] = yx[HALO : HALO + 8, :]
-        conv_first(b, t, yx, left, theirs, EXTRA, EXTRA)
-
-    def second(b, t):
-        end = ends[t] + (HALO if t == parts - 1 else 0)
-
-        def own(at):
-            pieces = [acts[s, b, pl.ds(at, tile), :].astype(jnp.float32) for s in range(4)]
-            hid1[pl.ds(at, tile), :] = activate(jnp.concatenate(pieces, axis=-1), 1)
-
-        each(begins[t], ends[t], own)
+            y, lambda p, q: hid1[p:q, :], lambda n, s: wv[1, :, n : n + s],
+            edges1[t], edges1[t + 1], taps * share, beside=beside,
+        )
+
+    def finish_second(b, t):
         if t == parts - 1:
-            pieces = [acts[s, b, rows : rows + HALO, :].astype(jnp.float32) for s in range(4)]
-            edge = jnp.concatenate(pieces, axis=-1)[0:8, :]
-            hid1[rows : rows + HALO, :] = activate(
-                jnp.concatenate([edge, jnp.zeros_like(edge)], axis=0), 1
-            )
-        product(
-            y, lambda p, q: hid1[p:q, :], lambda n, s: wv[1, :, n : n + s], 24, begins[t], end,
-            taps * share,
-        )
-        if t == parts - 1:
-            y[HALO : HALO + 8, :] = y[HALO + 8 + rows : HALO + 16 + rows, :]
-
-        def body(at):
-            value = acts[me, b, pl.ds(at, tile), :].astype(jnp.float32)
-            value = value + gather_taps(y, at, share, share)
-            last[b, pl.ds(at, tile), :] = value.astype(jnp.bfloat16)
-
-        each(max(begins[t] - tile, tile), rows if t == parts - 1 else ends[t] - tile, body)
-        if t == parts - 1:
-            body(0)
-
-    def out_first(b):
-        return pltpu.make_async_copy(acts.at[me, b, pl.ds(0, rows), :], out.at[0, b], osem.at[b])
-
-    cuts = (0, tile, ends[-2] - tile, rows)
+            close(y)
+        for u in outputs(edges1, t):
+            if u == rows - 32:
+                continue
+            at = held(u)
+            value = acts[me, b, at : at + tile, :].astype(jnp.float32)
+            value = value + gather_taps(y, u, share, share)
+            row = u + 32 if u < rows - 32 else u - (rows - 16)
+            last[b, row : row + tile, :] = value.astype(jnp.bfloat16)
+
+    def out_first(b, n):
+        begin, size, row = ((0, rows - 32, 32), (rows - 32, 32, 0))[n]
+        return pltpu.make_async_copy(
+            acts.at[me, b, pl.ds(begin, size), :], out.at[0, b, pl.ds(row, size)], osem.at[b, n]
+        )
+
+    cuts = (0, 32 + tile, edges1[-2] + 32 - tile, rows)
 
     def out_last(b, n):
         part = pl.ds(cuts[n], cuts[n + 1] - cuts[n])
@@ -488,9 +483,9 @@
 
     errands = {}
     for n in range(len(groups)):
-        errands.setdefault(1 + 2 * n, []).append(("own", 0, n))
+        errands.setdefault(2 + n, []).append(("own", 0, n))
         for d in range(1, planes):
-            errands.setdefault(min(5 + 4 * (d - 1) + n, count), []).append(("far", d, n))
+            errands.setdefault(min(2 + 3 * d + n, count), []).append(("far", d, n))
 
     def errand(e):
         kind, d, n = e
@@ -499,24 +494,70 @@
         else:
             spread_far(d, n)
 
+    gains.wait()
+    load_part(0).wait()
+    for work in norm_first(0, 0):
+        work()
+    enter()
+    for k in range(2):
+        weight(0, k).wait()
+    multiply_first(0, 0, head)
+    for other in range(1, micro):
+        load(other).start()
+    for k in range(taps):
+        weight(1, k).start()
+    for k in range(2, taps):
+        weight(0, k).wait()
+    load_part(1).wait()
+
     @pl.loop(0, micro)
     def _(b):
         for t in range(parts):
-            first(b, t)
+            if t == 1:
+
+                @pl.when(seq > 0)
+                def _():
+                    halo_up(b).wait_recv()
+
+                @pl.when(seq < nseq - 1)
+                def _():
+                    halo_down(b).wait_recv()
+
+            if t < parts - 1:
+                multiply_first(b, t, tail, norm_first(b, t + 1))
+                finish_first(b, t)
+                multiply_first(b, t + 1, head)
+            else:
+
+                @pl.when(b < micro - 1)
+                def _():
+                    load(b + 1).wait()
+                    multiply_first(b, t, tail, norm_first(b + 1, 0))
+                    finish_first(b, t)
+                    multiply_first(b + 1, 0, head)
+
+                @pl.when(b == micro - 1)
+                def _():
+                    multiply_first(b, t, tail)
+                    finish_first(b, t)
+
             at_step(b, t, {c: (c,) for c in range(3)}, direct)
             at_step(b, t, {p: (m,) for p, m in early.items()}, forward)
             at_step(b, t, errands, errand)
-        out_first(b).start()
+        for n in range(2):
+            out_first(b, n).start()
 
     for m in between[:1]:
         forward(m)
     for e in errands.get(count, ()):
         errand(e)
-    for m in between[1:]:
-        forward(m)
     for n in range(len(groups)):
         for at in range(planes):
             swapped(at, n).wait_recv()
+    for m in between[1:]:
+        forward(m)
+    extra(0, 0, slice(None))
+    finish_extra(0, 0)
     for k in range(taps):
         weight(1, k).wait()
 
@@ -524,9 +565,30 @@
     def _(b):
         for t in range(parts):
             at_step(b, t, late, forward)
-            extra(b, t)
             arrived(b, t)
-            second(b, t)
+            if t < parts - 1:
+                extra(b, t + 1, head, norm_second(b, t))
+                multiply_second(b, t)
+                extra(b, t + 1, tail)
+                finish_second(b, t)
+                finish_extra(b, t + 1)
+            else:
+
+                @pl.when(b < micro - 1)
+                def _():
+                    extra(b + 1, 0, head, norm_second(b, t))
+                    multiply_second(b, t)
+                    extra(b + 1, 0, tail)
+                    finish_second(b, t)
+                    finish_extra(b + 1, 0)
+
+                @pl.when(b == micro - 1)
+                def _():
+                    for work in norm_second(b, t):
+                        work()
+                    multiply_second(b, t)
+                    finish_second(b, t)
+
             if t == parts - 2:
                 out_last(b, 1).start()
         out_last(b, 0).start()
@@ -551,7 +613,8 @@
 
     @pl.loop(0, micro)
     def _(b):
-        out_first(b).wait()
+        for n in range(2):
+            out_first(b, n).wait()
         for n in range(3):
             out_last(b, n).wait()
 
@@ -561,6 +624,9 @@
     layers, taps, _, share = weights.shape
     span = rows + 2 * HALO
     count = len(chunk_ends(rows)) * micro
+    ends = chunk_ends(rows)
+    edges = [0] + [e + 32 for e in ends[:-1]] + [rows + 16]
+    sizes = [q - p for p, q in zip(edges, edges[1:])]
     planes = lax.axis_size("seq") // 2
     dma = pltpu.SemaphoreType.DMA
     hbm = pl.BlockSpec(memory_space=pltpu.HBM)
@@ -571,10 +637,10 @@
         out_specs=pl.BlockSpec(memory_space=pl.ANY),
         scratch_shapes=[
             pltpu.VMEM((micro, span, chans), jnp.bfloat16),
-            pltpu.VMEM((micro, rows + HALO, chans), jnp.bfloat16),
+            *(pltpu.VMEM((micro, n, chans), jnp.bfloat16) for n in sizes),
             pltpu.VMEM((rows + HALO, chans), jnp.bfloat16),
-            pltpu.VMEM((rows + 40, taps * share), jnp.float32),
-            pltpu.VMEM((rows + 40, taps * EXTRA), jnp.float32),
+            pltpu.VMEM((rows + 32, taps * share), jnp.float32),
+            pltpu.VMEM((rows + 32, taps * EXTRA), jnp.float32),
             pltpu.VMEM((2, chans, taps * share), jnp.bfloat16),
             pltpu.VMEM((chans, taps * EXTRA), jnp.bfloat16),
             pltpu.VMEM(gains.shape, jnp.float32),
@@ -582,12 +648,12 @@
             pltpu.VMEM((micro, rows, share), jnp.bfloat16),
             dma,
             dma((2, taps)),
-            dma((micro,)),
+            dma((micro + 1,)),
             dma((2, micro)),
             dma((2, micro)),
             dma((4, count)),
             dma((4, count)),
-            dma((micro,)),
+            dma((micro, 2)),
             dma((micro, 3)),
             dma((taps,)),
             dma((taps,)),

time: 70.3 us -> 66.7 us (0.949)
  Pallas kernels: 67.7 us -> 64.1 us
    pallas_call x1, Pallas kernels: 67.7 us -> 64.1 us  [fused(): pl.pallas_call(fused_kernel, out_shape=jax.ShapeDtypeStruct((layers, micr...]
where the time goes in v2:
time: 66.7 us; the launch traced here: 66.5 us
  Pallas kernels  64.1 us (96%)
  local copies, waits for them, and re-layouts  2.37 us (4%)
    pallas_call x1, Pallas kernels, fused(): pl.pallas_call(fused_kernel, out_shape=jax.ShapeDtypeStruct((layers, micr...  64.1 us
    unnamed x3, local copies, waits for them, and re-layouts  2.37 us

profile of v2, /device:TPU:0, one launch (start us, length us, event | category | flops | bytes accessed | tf_op | source)
XLA Modules:
  0.0 66.5 jit_solution(14917701139953900279)
XLA Ops:
  0.0 0.0 copy-start
  0.0 0.7 %copy-done = f32[2,1536]{1,0:T(2,128)S(1)} copy-done((f32[2,1536]{1,0:T(2,128)S(1)}, f32[2,1536]{1,0:T(2,128)}, u32[]{:S(2)}) %copy-start) | copy-done | bytes 12312
  0.7 64.1 %shard_map.37 = bf16[2,4,512,384]{3,2,1,0:T(8,128)(2,1)S(1)} custom-call(bf16[4,512,1536]{2,1,0:T(8,128)(2,1)} %x.1, bf16[2,5,1536,384]{3,2,1,0:T(8,128)(2,1)} %w.1, f32[2,1536]{1,0:T(2,128)S(1)} %copy-done), custom_call_target="tpu_custom_call" | custom-call | tf_op jit(solution)/shard_map/pallas_call | solution.py:633
  64.9 1.7 %copy.5 = bf16[2,4,512,384]{3,2,1,0:T(8,128)(2,1)} copy(bf16[2,4,512,384]{3,2,1,0:T(8,128)(2,1)S(1)} %shard_map.37) | data formatting | bytes 6291456
Async XLA Ops:
  0.0 0.7 %copy-start = (f32[2,1536]{1,0:T(2,128)S(1)}, f32[2,1536]{1,0:T(2,128)}, u32[]{:S(2)}) copy-start(f32[2,1536]{1,0:T(2,128)} %g.1) | copy-start | bytes 36868

commit v3 on v2

--- a/solution.py
+++ b/solution.py
@@ -72,11 +72,8 @@
 
 def schedule(count):
     early = {5 + 2 * m: m for m in range(3)}
-    between = list(range(len(early), min(len(early) + 2, count)))
-    rest = range(len(early) + len(between), count)
-    late = {}
-    for n, m in enumerate(rest):
-        late.setdefault(max(0, min(2 * n + 1, m - 1)), []).append(m)
+    between = [len(early)]
+    late = {m - 2: (m,) for m in range(len(early) + 1, count)}
     return early, between, late
 
 
@@ -292,10 +289,15 @@
             for b in range(micro):
                 halo_down(b).start()
 
+    def channels(way, whole):
+        if whole:
+            return ((0, share), (0, share), (2 * EXTRA, share), (0, 2 * EXTRA))[way]
+        return ((EXTRA, share), (0, share), (EXTRA, share), (0, EXTRA))[way]
+
     def send(origin, c, way, to):
         b, t = c // parts, c % parts
         size = ends[t] - begins[t]
-        low, high = ((EXTRA, share), (0, share), (EXTRA, share), (0, EXTRA))[way]
+        low, high = channels(way, b == 0)
         ref = acts.at[origin, b, pl.ds(begins[t], size), pl.ds(low, high - low)]
         return pltpu.make_async_remote_copy(
             src_ref=ref,
@@ -315,13 +317,18 @@
         send(left, c, 2, right).start()
         send(right, c, 1, right).wait_recv()
         send(right, c, 3, left).start()
-        if c + 3 < count:
-            direct(c + 3)
+        if c + 4 < count:
+            direct(c + 4)
 
     def arrived(b, t):
+        pl.when(b == 0)(lambda: arrived_in(b, t, True))
+        pl.when(b > 0)(lambda: arrived_in(b, t, False))
+
+    def arrived_in(b, t, whole):
         size = ends[t] - begins[t]
         c = b * parts + t
-        for way, low, high in ((2, EXTRA, share), (3, 0, EXTRA)):
+        for way in (2, 3):
+            low, high = channels(way, whole)
             ref = acts.at[over, b, pl.ds(begins[t], size), pl.ds(low, high - low)]
             pltpu.make_async_remote_copy(
                 src_ref=ref,
@@ -476,6 +483,11 @@
         part = pl.ds(cuts[n], cuts[n + 1] - cuts[n])
         return pltpu.make_async_copy(last.at[b, part], out.at[1, b, part], lsem.at[b, n])
 
+    def swaps_done():
+        for n in range(len(groups)):
+            for at in range(planes):
+                swapped(at, n).wait_recv()
+
     def at_step(b, t, table, act):
         for bb in range(micro):
             for m in table.get(bb * parts + t, ()):
@@ -483,9 +495,9 @@
 
     errands = {}
     for n in range(len(groups)):
-        errands.setdefault(2 + n, []).append(("own", 0, n))
+        errands.setdefault(3 + n, []).append(("own", 0, n))
         for d in range(1, planes):
-            errands.setdefault(min(2 + 3 * d + n, count), []).append(("far", d, n))
+            errands.setdefault(min(3 + 3 * d + n, count), []).append(("far", d, n))
 
     def errand(e):
         kind, d, n = e
@@ -541,53 +553,51 @@
                     multiply_first(b, t, tail)
                     finish_first(b, t)
 
-            at_step(b, t, {c: (c,) for c in range(3)}, direct)
+            at_step(b, t, {c: (c,) for c in range(4)}, direct)
             at_step(b, t, {p: (m,) for p, m in early.items()}, forward)
             at_step(b, t, errands, errand)
         for n in range(2):
             out_first(b, n).start()
 
-    for m in between[:1]:
+    for m in between:
         forward(m)
-    for e in errands.get(count, ()):
-        errand(e)
-    for n in range(len(groups)):
-        for at in range(planes):
-            swapped(at, n).wait_recv()
-    for m in between[1:]:
-        forward(m)
-    extra(0, 0, slice(None))
-    finish_extra(0, 0)
     for k in range(taps):
         weight(1, k).wait()
+
+    def step_second(b, t, more):
+        norms = norm_second(b, t)
+        for n in more:
+            extra(b + 1, n, head, norms)
+            norms = ()
+            if n != more[-1]:
+                extra(b + 1, n, tail)
+                finish_extra(b + 1, n)
+        for work in norms:
+            work()
+        multiply_second(b, t)
+        if more:
+            extra(b + 1, more[-1], tail)
+        finish_second(b, t)
+        if more:
+            finish_extra(b + 1, more[-1])
 
     @pl.loop(0, micro)
     def _(b):
         for t in range(parts):
             at_step(b, t, late, forward)
+            at_step(b, t, {1: errands.get(count, ())}, errand)
+            at_step(b, t, {1: (0,)}, lambda _: swaps_done())
             arrived(b, t)
-            if t < parts - 1:
-                extra(b, t + 1, head, norm_second(b, t))
-                multiply_second(b, t)
-                extra(b, t + 1, tail)
-                finish_second(b, t)
-                finish_extra(b, t + 1)
+            if t == 0:
+                pl.when((b > 0) & (b < micro - 1))(lambda: step_second(b, 0, (0,)))
+                pl.when((b == 0) | (b == micro - 1))(lambda: step_second(b, 0, ()))
+            elif t == 1:
+                pl.when(b == 0)(lambda: step_second(b, 1, (0, 1)))
+                pl.when((b > 0) & (b < micro - 1))(lambda: step_second(b, 1, (1,)))
+                pl.when(b == micro - 1)(lambda: step_second(b, 1, ()))
             else:
-
-                @pl.when(b < micro - 1)
-                def _():
-                    extra(b + 1, 0, head, norm_second(b, t))
-                    multiply_second(b, t)
-                    extra(b + 1, 0, tail)
-                    finish_second(b, t)
-                    finish_extra(b + 1, 0)
-
-                @pl.when(b == micro - 1)
-                def _():
-                    for work in norm_second(b, t):
-                        work()
-                    multiply_second(b, t)
-                    finish_second(b, t)
+                pl.when(b < micro - 1)(lambda: step_second(b, 2, (2,)))
+                pl.when(b == micro - 1)(lambda: step_second(b, 2, ()))
 
             if t == parts - 2:
                 out_last(b, 1).start()
@@ -673,7 +683,7 @@
     layers, taps, _, share = weights.shape
     nseq = lax.axis_size("seq")
     square = lax.axis_size("section") == 4 and layers == 2 and nseq % 2 == 0 and nseq > 2
-    wide = share % 128 == 0 and share > EXTRA and chans % (16 * nseq) == 0
+    wide = share % 128 == 0 and share > 2 * EXTRA and chans % (16 * nseq) == 0
     if square and wide and taps == 5 and micro > 1 and rows % 512 == 0:
         return fused(inputs, weights, gains)
     return plain(inputs, weights, gains)

time: 66.7 us -> 66.4 us (level)
  no operation moved by 1% of the time
where the time goes in v3:
time: 66.4 us; the launch traced here: 66.2 us
  Pallas kernels  63.8 us (96%)
  local copies, waits for them, and re-layouts  2.37 us (4%)
    pallas_call x1, Pallas kernels, fused(): pl.pallas_call(fused_kernel, out_shape=jax.ShapeDtypeStruct((layers, micr...  63.8 us
    unnamed x3, local copies, waits for them, and re-layouts  2.37 us

profile of v3, /device:TPU:0, one launch (start us, length us, event | category | flops | bytes accessed | tf_op | source)
XLA Modules:
  0.0 66.2 jit_solution(12977623816273973165)
XLA Ops:
  0.0 0.0 copy-start
  0.0 0.7 %copy-done = f32[2,1536]{1,0:T(2,128)S(1)} copy-done((f32[2,1536]{1,0:T(2,128)S(1)}, f32[2,1536]{1,0:T(2,128)}, u32[]{:S(2)}) %copy-start) | copy-done | bytes 12312
  0.7 63.8 %shard_map.37 = bf16[2,4,512,384]{3,2,1,0:T(8,128)(2,1)S(1)} custom-call(bf16[4,512,1536]{2,1,0:T(8,128)(2,1)} %x.1, bf16[2,5,1536,384]{3,2,1,0:T(8,128)(2,1)} %w.1, f32[2,1536]{1,0:T(2,128)S(1)} %copy-done), custom_call_target="tpu_custom_call" | custom-call | tf_op jit(solution)/shard_map/pallas_call | solution.py:643
  64.5 1.7 %copy.5 = bf16[2,4,512,384]{3,2,1,0:T(8,128)(2,1)} copy(bf16[2,4,512,384]{3,2,1,0:T(8,128)(2,1)S(1)} %shard_map.37) | data formatting | bytes 6291456
Async XLA Ops:
  0.0 0.7 %copy-start = (f32[2,1536]{1,0:T(2,128)S(1)}, f32[2,1536]{1,0:T(2,128)}, u32[]{:S(2)}) copy-start(f32[2,1536]{1,0:T(2,128)} %g.1) | copy-start | bytes 36868

commit v4 on v3

--- a/solution.py
+++ b/solution.py
@@ -78,8 +78,8 @@
 
 
 def fused_kernel(
-    x, w, g, out, xe, hid_a, hid_b, hid_c, hid1, y, yx, wv, wx, gv, acts, last,
-    gsem, wsem, xsem, hsend, hrecv, ssem, rsem, osem, lsem,
+    x, w, g, out, xe, hid_a, hid_b, hid_c, hid1, y, yx, wv, wx, gv, acts,
+    gsem, wsem, xsem, hsend, hrecv, ssem, rsem, osem,
     tsend, trecv, zsend, zrecv, psend, precv,
 ):
     micro, rows, chans = x.shape
@@ -469,19 +469,13 @@
             value = acts[me, b, at : at + tile, :].astype(jnp.float32)
             value = value + gather_taps(y, u, share, share)
             row = u + 32 if u < rows - 32 else u - (rows - 16)
-            last[b, row : row + tile, :] = value.astype(jnp.bfloat16)
+            out[1, b, row : row + tile, :] = value.astype(jnp.bfloat16)
 
     def out_first(b, n):
         begin, size, row = ((0, rows - 32, 32), (rows - 32, 32, 0))[n]
         return pltpu.make_async_copy(
             acts.at[me, b, pl.ds(begin, size), :], out.at[0, b, pl.ds(row, size)], osem.at[b, n]
         )
-
-    cuts = (0, 32 + tile, edges1[-2] + 32 - tile, rows)
-
-    def out_last(b, n):
-        part = pl.ds(cuts[n], cuts[n + 1] - cuts[n])
-        return pltpu.make_async_copy(last.at[b, part], out.at[1, b, part], lsem.at[b, n])
 
     def swaps_done():
         for n in range(len(groups)):
@@ -599,10 +593,6 @@
                 pl.when(b < micro - 1)(lambda: step_second(b, 2, (2,)))
                 pl.when(b == micro - 1)(lambda: step_second(b, 2, ()))
 
-            if t == parts - 2:
-                out_last(b, 1).start()
-        out_last(b, 0).start()
-        out_last(b, 2).start()
 
     @pl.when(seq < nseq - 1)
     def _():
@@ -625,8 +615,6 @@
     def _(b):
         for n in range(2):
             out_first(b, n).wait()
-        for n in range(3):
-            out_last(b, n).wait()
 
 
 def fused(inputs, weights, gains):
@@ -644,7 +632,7 @@
         fused_kernel,
         out_shape=jax.ShapeDtypeStruct((layers, micro, rows, share), jnp.bfloat16),
         in_specs=[hbm, hbm, hbm],
-        out_specs=pl.BlockSpec(memory_space=pl.ANY),
+        out_specs=pl.BlockSpec(memory_space=pltpu.VMEM),
         scratch_shapes=[
             pltpu.VMEM((micro, span, chans), jnp.bfloat16),
             *(pltpu.VMEM((micro, n, chans), jnp.bfloat16) for n in sizes),
@@ -655,7 +643,6 @@
             pltpu.VMEM((chans, taps * EXTRA), jnp.bfloat16),
             pltpu.VMEM(gains.shape, jnp.float32),
             pltpu.VMEM((4, micro, rows + HALO, share), jnp.bfloat16),
-            pltpu.VMEM((micro, rows, share), jnp.bfloat16),
             dma,
             dma((2, taps)),
             dma((micro + 1,)),
@@ -664,7 +651,6 @@
             dma((4, count)),
             dma((4, count)),
             dma((micro, 2)),
-            dma((micro, 3)),
             dma((taps,)),
             dma((taps,)),
             dma((2, planes, 2)),

time: 66.4 us -> 65.4 us (0.985)
  Pallas kernels: 63.8 us -> 62.8 us
    pallas_call x1, Pallas kernels: 63.8 us -> 62.8 us  [fused(): pl.pallas_call(fused_kernel, out_shape=jax.ShapeDtypeStruct((layers, micr...]
where the time goes in v4:
time: 65.4 us; the launch traced here: 65.2 us
  Pallas kernels  62.8 us (96%)
  local copies, waits for them, and re-layouts  2.37 us (4%)
    pallas_call x1, Pallas kernels, fused(): pl.pallas_call(fused_kernel, out_shape=jax.ShapeDtypeStruct((layers, micr...  62.8 us
    unnamed x3, local copies, waits for them, and re-layouts  2.37 us

profile of v4, /device:TPU:0, one launch (start us, length us, event | category | flops | bytes accessed | tf_op | source)
XLA Modules:
  0.0 65.2 jit_solution(3761053676005969734)
XLA Ops:
  0.0 0.0 copy-start
  0.0 0.7 %copy-done = f32[2,1536]{1,0:T(2,128)S(1)} copy-done((f32[2,1536]{1,0:T(2,128)S(1)}, f32[2,1536]{1,0:T(2,128)}, u32[]{:S(2)}) %copy-start) | copy-done | bytes 12312
  0.7 62.8 %shard_map.37 = bf16[2,4,512,384]{3,2,1,0:T(8,128)(2,1)S(1)} custom-call(bf16[4,512,1536]{2,1,0:T(8,128)(2,1)} %x.1, bf16[2,5,1536,384]{3,2,1,0:T(8,128)(2,1)} %w.1, f32[2,1536]{1,0:T(2,128)S(1)} %copy-done), custom_call_target="tpu_custom_call" | custom-call | tf_op jit(solution)/shard_map/pallas_call | solution.py:631
  63.5 1.7 %copy.5 = bf16[2,4,512,384]{3,2,1,0:T(8,128)(2,1)} copy(bf16[2,4,512,384]{3,2,1,0:T(8,128)(2,1)S(1)} %shard_map.37) | data formatting | bytes 6291456
Async XLA Ops:
  0.0 0.7 %copy-start = (f32[2,1536]{1,0:T(2,128)S(1)}, f32[2,1536]{1,0:T(2,128)}, u32[]{:S(2)}) copy-start(f32[2,1536]{1,0:T(2,128)} %g.1) | copy-start | bytes 36868

commit v5 on v4

--- a/solution.py
+++ b/solution.py
@@ -317,8 +317,10 @@
         send(left, c, 2, right).start()
         send(right, c, 1, right).wait_recv()
         send(right, c, 3, left).start()
-        if c + 4 < count:
-            direct(c + 4)
+        for n in range(4, count):
+            ahead = 2 if n == count - 1 else 3 if n == count - 2 else 4
+            if c == n - ahead:
+                direct(n)
 
     def arrived(b, t):
         pl.when(b == 0)(lambda: arrived_in(b, t, True))

time: 65.4 us -> 65.5 us (level)
  no operation moved by 1% of the time
where the time goes in v5:
time: 65.5 us; the launch traced here: 65.3 us
  Pallas kernels  62.9 us (96%)
  local copies, waits for them, and re-layouts  2.37 us (4%)
    pallas_call x1, Pallas kernels, fused(): pl.pallas_call(fused_kernel, out_shape=jax.ShapeDtypeStruct((layers, micr...  62.9 us
    unnamed x3, local copies, waits for them, and re-layouts  2.37 us

profile of v5, /device:TPU:0, one launch (start us, length us, event | category | flops | bytes accessed | tf_op | source)
XLA Modules:
  0.0 65.3 jit_solution(571927481322177231)
XLA Ops:
  0.0 0.0 copy-start
  0.0 0.7 %copy-done = f32[2,1536]{1,0:T(2,128)S(1)} copy-done((f32[2,1536]{1,0:T(2,128)S(1)}, f32[2,1536]{1,0:T(2,128)}, u32[]{:S(2)}) %copy-start) | copy-done | bytes 12312
  0.7 62.9 %shard_map.37 = bf16[2,4,512,384]{3,2,1,0:T(8,128)(2,1)S(1)} custom-call(bf16[4,512,1536]{2,1,0:T(8,128)(2,1)} %x.1, bf16[2,5,1536,384]{3,2,1,0:T(8,128)(2,1)} %w.1, f32[2,1536]{1,0:T(2,128)S(1)} %copy-done), custom_call_target="tpu_custom_call" | custom-call | tf_op jit(solution)/shard_map/pallas_call | solution.py:633
  63.7 1.7 %copy.5 = bf16[2,4,512,384]{3,2,1,0:T(8,128)(2,1)} copy(bf16[2,4,512,384]{3,2,1,0:T(8,128)(2,1)S(1)} %shard_map.37) | data formatting | bytes 6291456
Async XLA Ops:
  0.0 0.7 %copy-start = (f32[2,1536]{1,0:T(2,128)S(1)}, f32[2,1536]{1,0:T(2,128)}, u32[]{:S(2)}) copy-start(f32[2,1536]{1,0:T(2,128)} %g.1) | copy-start | bytes 36868
